TPU v7x, 512 devices: a whole 4x8x8 slice. The times are simulated.
512 devices in a mesh: box: 64 (over y, x, core), samp: 8 (over z).
Axes of the slice: x: 4, y: 8, z: 8, core: 2. Of those that a mesh axis runs over, the one named last changes fastest.
Arguments:
- currents: bfloat16 [2048, 8, 128], P(('box', 'samp')), may hold values from -6 to 6
- radiation: bfloat16 [2048, 2, 2, 512, 128], P(('box', 'samp')), may hold values from -0.1875 to 0.1875
- near_blocks: bfloat16 [2048, 8, 2, 128, 128], P(('box', 'samp')), may hold values from -0.125 to 0.125
- near_src: int32 [2048, 8], P(('box', 'samp')), may hold values from 0 to 2047, as said below
- leaf_parent: int32 [2048], P('box'), may hold values from 0 to 1023, as said below
- leaf_shift: int32 [2048], P('box'), may hold values from 0 to 7
- shift_table: bfloat16 [8, 2, 8192], P(None, None, 'samp'), may hold values from -4 to 4
- interp_idx: int32 [64, 2], P('samp'), may hold values from 0 to 3, as said below
- interp_val: bfloat16 [64, 2, 128, 128], P('samp'), may hold values from -0.375 to 0.375
- top_src: int32 [1024, 16], P('box'), may hold values from 0 to 1023, as said below
- top_disp: int32 [1024, 16], P('box'), may hold values from 0 to 31
- trans_table: bfloat16 [32, 2, 8192], P(None, None, 'samp'), may hold values from -1 to 1
Outputs:
- matvec: float32 [2048, 8, 128], P(('box', 'samp'))
Inputs may be any that keep to these rules, and one draw needn't show every extreme that they name: `near_src`: entry 0 of a leaf's row is the leaf itself; every entry lies in the 4 leaves of the leaf's own device or of the devices just before and after it in box+samp order (leaves numbered box-major), and these ends are reached. `leaf_parent`: the parent of leaf l lies in its box group: its value divided by 16 equals l divided by 32. `interp_idx`: the 2 entries of a row differ. `top_src`: a source of top box t is another box of t's group (t // 16), or one of the last 8 boxes of the group before it, or one of the first 8 boxes of the group after it; both rims are reached.
All inputs are finite; a program needn't handle non-finite values.
Results may differ from a plain program's by a relative error of at most 0.013.
Values may be sent and summed in bfloat16 or wider, within the bound.
A program may use at most 64 MiB of HBM per device.

v0:
```python
import jax
import jax.numpy as jnp
from jax import lax
from jax.sharding import PartitionSpec as P

HIGHEST = lax.Precision.HIGHEST


def with_halo(cells, sides, width):
    for axis, dim in sides:
        count = lax.axis_size(axis)
        ends = count - 1
        head = lax.slice_in_dim(cells, 0, width, axis=dim)
        tail = lax.slice_in_dim(cells, cells.shape[dim] - width, cells.shape[dim], axis=dim)
        cells = jnp.concatenate(
            [
                lax.ppermute(tail, axis, [(i, (i + 1) % count) for i in range(ends)]),
                cells,
                lax.ppermute(head, axis, [((i + 1) % count, i) for i in range(ends)]),
            ],
            axis=dim,
        )
    return cells


def complex_mul(a_real, a_imag, b_real, b_imag):
    return (a_real * b_real - a_imag * b_imag, a_real * b_imag + a_imag * b_real)


def contract(form, first_op, second_op):
    return jnp.einsum(form, first_op, second_op, preferred_element_type=jnp.float32)


def per_device(
    currents,
    radiation,
    near_blocks,
    near_src,
    leaf_parent,
    leaf_shift,
    shift_table,
    interp_idx,
    interp_val,
    top_src,
    top_disp,
    trans_table,
):
    leaf_count = currents.shape[0]
    half_comp = currents.shape[1]
    excite = half_comp // 2
    comps = 2 * half_comp
    samp_count = lax.axis_size("samp")
    group_index = lax.axis_index("box")
    first_leaf = (group_index * samp_count + lax.axis_index("samp")) * leaf_count
    top_count = top_src.shape[0]
    block_size = interp_val.shape[2]
    leaf_samples = radiation.shape[3]
    in_blocks = leaf_samples // block_size
    local_blocks = interp_val.shape[0]
    local_samples = local_blocks * block_size
    neighbours = with_halo(currents, ((("box", "samp"), 0),), leaf_count)
    rad_real = radiation[:, :, 0]
    rad_imag = radiation[:, :, 1]
    form_out = "lpqu,leu->lpeq"
    out_real = contract(form_out, rad_real, currents[:, :excite]) - contract(
        form_out, rad_imag, currents[:, excite:]
    )
    out_imag = contract(form_out, rad_real, currents[:, excite:]) + contract(
        form_out, rad_imag, currents[:, :excite]
    )
    patterns = jnp.concatenate(
        [
            out_real.reshape(leaf_count, half_comp, leaf_samples),
            out_imag.reshape(leaf_count, half_comp, leaf_samples),
        ],
        axis=1,
    ).astype(jnp.bfloat16)
    piece = lax.all_gather(patterns, "samp", axis=0, tiled=True)
    piece_rows = piece.shape[0]
    picked = piece.reshape(piece_rows, comps, in_blocks, block_size)[:, :, interp_idx, :]
    moved_rows = contract("lcbri,brki->lcbk", picked, interp_val)
    moved = moved_rows.reshape(piece_rows, comps, local_samples)
    shift_onehot = (leaf_shift[:, None] == jnp.arange(shift_table.shape[0])[None, :]).astype(
        jnp.bfloat16
    )
    shift_rows = contract("ln,nrk->lrk", shift_onehot, shift_table)
    shift_real = shift_rows[:, 0:1]
    shift_imag = shift_rows[:, 1:2]
    up_real, up_imag = complex_mul(
        moved[:, :half_comp], moved[:, half_comp:], shift_real, shift_imag
    )
    shifted = jnp.concatenate([up_real, up_imag], axis=1)
    parent_local = leaf_parent - group_index * top_count
    member = parent_local[None, :] == jnp.arange(top_count)[:, None]
    top_patterns = jnp.einsum(
        "tl,lck->tck", member.astype(jnp.float32), shifted, precision=HIGHEST
    ).astype(jnp.bfloat16)
    padded = with_halo(top_patterns, (("box", 0),), top_count)
    base_index = group_index * top_count - top_count
    disp_count = trans_table.shape[0]

    def add_entry(entry, total):
        source_rows = jnp.take(padded, top_src[:, entry] - base_index, axis=0).astype(jnp.float32)
        disp_onehot = (top_disp[:, entry][:, None] == jnp.arange(disp_count)[None, :]).astype(
            jnp.bfloat16
        )
        coeff = contract("tn,nrk->trk", disp_onehot, trans_table)
        part_real, part_imag = complex_mul(
            coeff[:, 0:1], coeff[:, 1:2], source_rows[:, :half_comp], source_rows[:, half_comp:]
        )
        return total + jnp.concatenate([part_real, part_imag], axis=1)

    incoming = lax.fori_loop(
        0, top_src.shape[1], add_entry, jnp.zeros((top_count, comps, local_samples), jnp.float32)
    ).astype(jnp.bfloat16)
    spread = contract("tl,tck->lck", member.astype(jnp.bfloat16), incoming)
    down_real, down_imag = complex_mul(
        shift_real, -shift_imag, spread[:, :half_comp], spread[:, half_comp:]
    )
    down = jnp.concatenate([down_real, down_imag], axis=1).astype(jnp.bfloat16)
    block_onehot = (interp_idx[:, :, None] == jnp.arange(in_blocks)[None, None, :]).astype(
        jnp.float32
    )
    parts = contract(
        "lcbk,brki->lcbri",
        down.reshape(leaf_count * lax.axis_size("samp"), comps, local_blocks, block_size),
        interp_val,
    )
    folded = jnp.einsum("lcbri,brq->lcqi", parts, block_onehot, precision=HIGHEST)
    far = lax.psum_scatter(
        folded.reshape(leaf_count * lax.axis_size("samp"), comps, leaf_samples).astype(
            jnp.bfloat16
        ),
        "samp",
        scatter_dimension=0,
        tiled=True,
    )
    far_real = far[:, :half_comp].reshape(leaf_count, 2, excite, leaf_samples)
    far_imag = far[:, half_comp:].reshape(leaf_count, 2, excite, leaf_samples)
    form_back = "lpqu,lpeq->leu"
    recv_real = contract(form_back, rad_real, far_real) + contract(form_back, rad_imag, far_imag)
    recv_imag = contract(form_back, rad_real, far_imag) - contract(form_back, rad_imag, far_real)
    near_rows = jnp.take(neighbours, near_src - first_leaf + leaf_count, axis=0)
    block_real = near_blocks[:, :, 0]
    block_imag = near_blocks[:, :, 1]
    form_near = "lnuv,lnev->leu"
    near_real = contract(form_near, block_real, near_rows[:, :, :excite]) - contract(
        form_near, block_imag, near_rows[:, :, excite:]
    )
    near_imag = contract(form_near, block_real, near_rows[:, :, excite:]) + contract(
        form_near, block_imag, near_rows[:, :, :excite]
    )
    return jnp.concatenate([recv_real + near_real, recv_imag + near_imag], axis=1)


def solution(mesh):
    placed = (
        P(("box", "samp"), None, None),
        P(("box", "samp"), None, None, None, None),
        P(("box", "samp"), None, None, None, None),
        P(("box", "samp"), None),
        P("box"),
        P("box"),
        P(None, None, "samp"),
        P("samp", None),
        P("samp", None, None, None),
        P("box", None),
        P("box", None),
        P(None, None, "samp"),
    )
    return jax.shard_map(
        per_device,
        mesh=mesh,
        in_specs=placed,
        out_specs=P(("box", "samp"), None, None),
        check_vma=False,
    )
```

profile of v0, /device:TPU:2, one launch (start us, length us, event | category | flops | bytes accessed | tf_op | source)
XLA Modules:
  0.0 176.0 jit_solution(13195029039709390717)
XLA Ops:
  6.6 1.8 %fusion.46 = f32[4,4,2,512]{3,1,2,0:T(4,128)S(1)} fusion(bf16[4,2,2,512,128]{4,3,2,1,0:T(8,128)(2,1)} %param.15, bf16[4,8,128]{2,1,0:T(8,128)(2,1)} %param.14), kind=kOutput, calls=%fused_computation.65 | convolution fusion | flops 4194304 | bytes 1118208 | tf_op jit(solution)/shard_map/lpqu,leu->lpeq/dot_general | solution.py:31
  8.4 1.6 fusion.44
  11.1 31.6 %all_gather.3 = bf16[32,16,512]{2,1,0:T(8,128)(2,1)S(1)} all-gather(bf16[4,16,512]{2,1,0:T(8,128)(2,1)S(1)} %pad_maximum_fusion.1), channel_id=1, replica_groups=mesh['box'=64,'samp'=8] {'samp'}, dimensions={0}, use_global_device_ids=true | all-gather | bytes 589824 | tf_op jit(solution)/shard_map/all_gather | solution.py:78
  44.9 2.5 %copy.92 = f32[32,16,8,128]{3,2,0,1:T(8,128)} copy(f32[32,16,8,128]{3,1,0,2:T(8,128)S(1)} %convolution_bitcast_fusion.1) | data formatting | bytes 4194304 | tf_op jit(solution)/shard_map/reshape | solution.py:82
  47.4 1.7 reshape.96
  50.4 1.9 %collective-permute-start = (bf16[16,16,1024]{2,0,1:T(8,128)(2,1)S(1)}, bf16[16,16,1024]{2,0,1:T(8,128)(2,1)S(1)}, u32[]{:S(2)}, u32[]{:S(2)}) collective-permute-start(bf16[16,16,1024]{2,0,1:T(8,128)(2,1)S(1)} %fusion.16), channel_id=1, source_target_pairs={{0,8},{8,16},{16,24},{24,32},{32,40},{40,48},{48,56},{56,64},{64,7... | collective-permute-start | bytes 1572872 | tf_op jit(solution)/shard_map/ppermute | solution.py:17
  52.3 3.8 %collective-permute-start.1 = (bf16[16,16,1024]{2,0,1:T(8,128)(2,1)S(1)}, bf16[16,16,1024]{2,0,1:T(8,128)(2,1)}, u32[]{:S(2)}, u32[]{:S(2)}) collective-permute-start(bf16[16,16,1024]{2,0,1:T(8,128)(2,1)S(1)} %fusion.16), channel_id=1, source_target_pairs={{8,0},{16,8},{24,16},{32,24},{40,32},{48,40},{56,48},{64,56},{72,6... | collective-permute-start | bytes 1572872 | tf_op jit(solution)/shard_map/ppermute | solution.py:19
  56.3 4.5 %collective-permute-done = bf16[16,16,1024]{2,0,1:T(8,128)(2,1)S(1)} collective-permute-done((bf16[16,16,1024]{2,0,1:T(8,128)(2,1)S(1)}, bf16[16,16,1024]{2,0,1:T(8,128)(2,1)S(1)}, u32[]{:S(2)}, u32[]{:S(2)}) %collective-permute-start) | collective-permute-done | bytes 524320 | tf_op jit(solution)/shard_map/ppermute | solution.py:17
  60.9 1.8 collective-permute-done.1
  63.8 2.0 %copy.70 = bf16[48,16,1024]{2,1,0:T(8,128)(2,1)} copy(bf16[48,16,1024]{2,0,1:T(8,128)(2,1)S(1)} %pad_maximum_fusion) | data formatting | bytes 3145728
  65.9 48.1 %while.14 = (s32[]{:T(128)}, f32[16,16,1024]{2,1,0:T(8,128)S(1)}, s32[16,16]{0,1:T(8,128)S(1)}, bf16[32,2,1024]{2,0,1:T(8,128)(2,1)S(1)}, s32[16,16]{0,1:T(8,128...) while((s32[]{:T(128)}, f32[16,16,1024]{2,1,0:T(8,128)S(1)}, ...), condition=%wide.region_1.0_spmd.clone, body=%wide.region_0.1_spmd.clone.sunk | while | flops 4195955 | bytes 8524371 | solution.py:113
  65.9 2.0 %gather_fusion = bf16[16,16,1024]{2,1,0:T(8,128)(2,1)S(1)} fusion(bf16[48,16,1024]{2,1,0:T(8,128)(2,1)} %get-tuple-element.292, s32[1024]{0:T(1024)S(1)} %pad_clamp_fusion.4), kind=kCustom, calls=%fused_computation.clone.clone.1 | custom fusion | bytes 1048640 | tf_op jit(solution)/shard_map/while/body/eval_jaxpr/jit(_take)/gather | solution.py:103
  68.9 2.0 %gather_fusion = bf16[16,16,1024]{2,1,0:T(8,128)(2,1)S(1)} fusion(bf16[48,16,1024]{2,1,0:T(8,128)(2,1)} %get-tuple-element.292, s32[1024]{0:T(1024)S(1)} %pad_clamp_fusion.4), kind=kCustom, calls=%fused_computation.clone.clone.1 | custom fusion | bytes 1048640 | tf_op jit(solution)/shard_map/while/body/eval_jaxpr/jit(_take)/gather | solution.py:103
  71.9 2.0 %gather_fusion = bf16[16,16,1024]{2,1,0:T(8,128)(2,1)S(1)} fusion(bf16[48,16,1024]{2,1,0:T(8,128)(2,1)} %get-tuple-element.292, s32[1024]{0:T(1024)S(1)} %pad_clamp_fusion.4), kind=kCustom, calls=%fused_computation.clone.clone.1 | custom fusion | bytes 1048640 | tf_op jit(solution)/shard_map/while/body/eval_jaxpr/jit(_take)/gather | solution.py:103
  74.9 2.0 %gather_fusion = bf16[16,16,1024]{2,1,0:T(8,128)(2,1)S(1)} fusion(bf16[48,16,1024]{2,1,0:T(8,128)(2,1)} %get-tuple-element.292, s32[1024]{0:T(1024)S(1)} %pad_clamp_fusion.4), kind=kCustom, calls=%fused_computation.clone.clone.1 | custom fusion | bytes 1048640 | tf_op jit(solution)/shard_map/while/body/eval_jaxpr/jit(_take)/gather | solution.py:103
  77.9 2.0 %gather_fusion = bf16[16,16,1024]{2,1,0:T(8,128)(2,1)S(1)} fusion(bf16[48,16,1024]{2,1,0:T(8,128)(2,1)} %get-tuple-element.292, s32[1024]{0:T(1024)S(1)} %pad_clamp_fusion.4), kind=kCustom, calls=%fused_computation.clone.clone.1 | custom fusion | bytes 1048640 | tf_op jit(solution)/shard_map/while/body/eval_jaxpr/jit(_take)/gather | solution.py:103
  80.9 2.0 %gather_fusion = bf16[16,16,1024]{2,1,0:T(8,128)(2,1)S(1)} fusion(bf16[48,16,1024]{2,1,0:T(8,128)(2,1)} %get-tuple-element.292, s32[1024]{0:T(1024)S(1)} %pad_clamp_fusion.4), kind=kCustom, calls=%fused_computation.clone.clone.1 | custom fusion | bytes 1048640 | tf_op jit(solution)/shard_map/while/body/eval_jaxpr/jit(_take)/gather | solution.py:103
  83.9 2.0 %gather_fusion = bf16[16,16,1024]{2,1,0:T(8,128)(2,1)S(1)} fusion(bf16[48,16,1024]{2,1,0:T(8,128)(2,1)} %get-tuple-element.292, s32[1024]{0:T(1024)S(1)} %pad_clamp_fusion.4), kind=kCustom, calls=%fused_computation.clone.clone.1 | custom fusion | bytes 1048640 | tf_op jit(solution)/shard_map/while/body/eval_jaxpr/jit(_take)/gather | solution.py:103
  86.9 2.0 %gather_fusion = bf16[16,16,1024]{2,1,0:T(8,128)(2,1)S(1)} fusion(bf16[48,16,1024]{2,1,0:T(8,128)(2,1)} %get-tuple-element.292, s32[1024]{0:T(1024)S(1)} %pad_clamp_fusion.4), kind=kCustom, calls=%fused_computation.clone.clone.1 | custom fusion | bytes 1048640 | tf_op jit(solution)/shard_map/while/body/eval_jaxpr/jit(_take)/gather | solution.py:103
  90.0 2.0 %gather_fusion = bf16[16,16,1024]{2,1,0:T(8,128)(2,1)S(1)} fusion(bf16[48,16,1024]{2,1,0:T(8,128)(2,1)} %get-tuple-element.292, s32[1024]{0:T(1024)S(1)} %pad_clamp_fusion.4), kind=kCustom, calls=%fused_computation.clone.clone.1 | custom fusion | bytes 1048640 | tf_op jit(solution)/shard_map/while/body/eval_jaxpr/jit(_take)/gather | solution.py:103
  93.0 2.0 %gather_fusion = bf16[16,16,1024]{2,1,0:T(8,128)(2,1)S(1)} fusion(bf16[48,16,1024]{2,1,0:T(8,128)(2,1)} %get-tuple-element.292, s32[1024]{0:T(1024)S(1)} %pad_clamp_fusion.4), kind=kCustom, calls=%fused_computation.clone.clone.1 | custom fusion | bytes 1048640 | tf_op jit(solution)/shard_map/while/body/eval_jaxpr/jit(_take)/gather | solution.py:103
  96.0 2.0 %gather_fusion = bf16[16,16,1024]{2,1,0:T(8,128)(2,1)S(1)} fusion(bf16[48,16,1024]{2,1,0:T(8,128)(2,1)} %get-tuple-element.292, s32[1024]{0:T(1024)S(1)} %pad_clamp_fusion.4), kind=kCustom, calls=%fused_computation.clone.clone.1 | custom fusion | bytes 1048640 | tf_op jit(solution)/shard_map/while/body/eval_jaxpr/jit(_take)/gather | solution.py:103
  99.0 2.0 %gather_fusion = bf16[16,16,1024]{2,1,0:T(8,128)(2,1)S(1)} fusion(bf16[48,16,1024]{2,1,0:T(8,128)(2,1)} %get-tuple-element.292, s32[1024]{0:T(1024)S(1)} %pad_clamp_fusion.4), kind=kCustom, calls=%fused_computation.clone.clone.1 | custom fusion | bytes 1048640 | tf_op jit(solution)/shard_map/while/body/eval_jaxpr/jit(_take)/gather | solution.py:103
  102.0 2.0 %gather_fusion = bf16[16,16,1024]{2,1,0:T(8,128)(2,1)S(1)} fusion(bf16[48,16,1024]{2,1,0:T(8,128)(2,1)} %get-tuple-element.292, s32[1024]{0:T(1024)S(1)} %pad_clamp_fusion.4), kind=kCustom, calls=%fused_computation.clone.clone.1 | custom fusion | bytes 1048640 | tf_op jit(solution)/shard_map/while/body/eval_jaxpr/jit(_take)/gather | solution.py:103
  105.0 2.0 %gather_fusion = bf16[16,16,1024]{2,1,0:T(8,128)(2,1)S(1)} fusion(bf16[48,16,1024]{2,1,0:T(8,128)(2,1)} %get-tuple-element.292, s32[1024]{0:T(1024)S(1)} %pad_clamp_fusion.4), kind=kCustom, calls=%fused_computation.clone.clone.1 | custom fusion | bytes 1048640 | tf_op jit(solution)/shard_map/while/body/eval_jaxpr/jit(_take)/gather | solution.py:103
  108.0 2.0 %gather_fusion = bf16[16,16,1024]{2,1,0:T(8,128)(2,1)S(1)} fusion(bf16[48,16,1024]{2,1,0:T(8,128)(2,1)} %get-tuple-element.292, s32[1024]{0:T(1024)S(1)} %pad_clamp_fusion.4), kind=kCustom, calls=%fused_computation.clone.clone.1 | custom fusion | bytes 1048640 | tf_op jit(solution)/shard_map/while/body/eval_jaxpr/jit(_take)/gather | solution.py:103
  111.0 2.0 %gather_fusion = bf16[16,16,1024]{2,1,0:T(8,128)(2,1)S(1)} fusion(bf16[48,16,1024]{2,1,0:T(8,128)(2,1)} %get-tuple-element.292, s32[1024]{0:T(1024)S(1)} %pad_clamp_fusion.4), kind=kCustom, calls=%fused_computation.clone.clone.1 | custom fusion | bytes 1048640 | tf_op jit(solution)/shard_map/while/body/eval_jaxpr/jit(_take)/gather | solution.py:103
  116.5 4.0 %fusion.19 = bf16[32,16,4,128]{3,2,1,0:T(4,128)(2,1)S(1)} fusion(f32[32,16,8,2,128]{4,1,3,0,2:T(8,128)S(1)} %convolution_bitcast_fusion, s32[8,2]{0,1:T(2,128)S(1)} %copy-done.9), kind=kOutput, calls=%fused_computation.29 | convolution fusion | flops 50593856 | bytes 4718656 | tf_op jit(solution)/shard_map/lcbri,brq->lcqi/dot_general | solution.py:129
  121.6 3.7 %collective-permute-start.2 = (bf16[4,8,128]{2,1,0:T(8,128)(2,1)S(1)}, bf16[4,8,128]{2,1,0:T(8,128)(2,1)S(1)}, u32[]{:S(2)}, u32[]{:S(2)}) collective-permute-start(bf16[4,8,128]{2,1,0:T(8,128)(2,1)S(1)} %copy-done.4), channel_id=1, source_target_pairs={{0,1},{1,2},{2,3},{3,4},{4,5},{5,6},{6,7},{7,8},{8,9},{9,10},{10,1... | collective-permute-start | bytes 24584 | tf_op jit(solution)/shard_map/ppermute | solution.py:17
  125.3 4.6 %collective-permute-start.3 = (bf16[4,8,128]{2,1,0:T(8,128)(2,1)S(1)}, bf16[4,8,128]{2,1,0:T(8,128)(2,1)S(1)}, u32[]{:S(2)}, u32[]{:S(2)}) collective-permute-start(bf16[4,8,128]{2,1,0:T(8,128)(2,1)S(1)} %copy-done.4), channel_id=1, source_target_pairs={{1,0},{2,1},{3,2},{4,3},{5,4},{6,5},{7,6},{8,7},{9,8},{10,9},{11,1... | collective-permute-start | bytes 24584 | tf_op jit(solution)/shard_map/ppermute | solution.py:19
  133.5 1.6 convolution_bitcast_fusion.3
  135.2 29.9 %reduce-scatter.2.cloned.1.call-done = bf16[4,16,512]{2,1,0:T(8,128)(2,1)} async-done(((bf16[32,16,512]{2,1,0:T(8,128)(2,1)}), bf16[4,16,512]{2,1,0:T(8,128)(2,1)}) %reduce-scatter.2.cloned.1.call-update) | async-done | bytes 65552 | tf_op jit(solution)/shard_map/reduce_scatter | solution.py:130
  (206 shorter events, 31.9 us)
Async XLA Ops:
  6.5 37.6 %copy-start = (bf16[8,2,128,128]{3,2,1,0:T(8,128)(2,1)S(1)}, bf16[8,2,128,128]{3,2,1,0:T(8,128)(2,1)}, u32[]{:S(2)}) copy-start(bf16[8,2,128,128]{3,2,1,0:T(8,128)(2,1)} %param.22) | copy-start | bytes 1572868
  6.5 3.7 %copy-start.4 = (bf16[4,8,128]{2,1,0:T(8,128)(2,1)S(1)}, bf16[4,8,128]{2,1,0:T(8,128)(2,1)}, u32[]{:S(2)}) copy-start(bf16[4,8,128]{2,1,0:T(8,128)(2,1)} %param.14) | copy-start | bytes 24580
  6.5 3.7 %copy-start.1 = (bf16[4,2,2,512,128]{4,3,2,1,0:T(8,128)(2,1)S(1)}, bf16[4,2,2,512,128]{4,3,2,1,0:T(8,128)(2,1)}, u32[]{:S(2)}) copy-start(bf16[4,2,2,512,128]{4,3,2,1,0:T(8,128)(2,1)} %param.15) | copy-start | bytes 6291460
  6.5 3.4 %copy-start.11 = (s32[32]{0:T(128)S(1)}, s32[32]{0:T(128)}, u32[]{:S(2)}) copy-start(s32[32]{0:T(128)} %param.19) | copy-start | bytes 388
  6.5 3.4 %copy-start.6 = (bf16[8,2,1024]{2,1,0:T(2,128)(2,1)S(1)}, bf16[8,2,1024]{2,1,0:T(2,128)(2,1)}, u32[]{:S(2)}) copy-start(bf16[8,2,1024]{2,1,0:T(2,128)(2,1)} %param.20) | copy-start | bytes 98308
  6.5 158.5 %reduce-scatter.2.cloned.1.call-start = ((), (), s32[]{:S(2)}) async-start(), calls=%async_computation.1 | async-start | bytes 589824 | tf_op jit(solution)/shard_map/reduce_scatter | solution.py:130
  10.3 32.6 %copy-start.9 = (s32[8,2]{0,1:T(2,128)S(1)}, s32[8,2]{0,1:T(2,128)}, u32[]{:S(2)}) copy-start(s32[8,2]{0,1:T(2,128)} %param.21) | copy-start | bytes 196
  47.4 1.7 copy-start.12
  49.5 6.7 %copy-start.5 = (bf16[32,2,1024]{2,1,0:T(2,128)(2,1)S(1)}, bf16[32,2,1024]{2,1,0:T(2,128)(2,1)}, u32[]{:S(2)}) copy-start(bf16[32,2,1024]{2,1,0:T(2,128)(2,1)} %param.25) | copy-start | bytes 393220
  49.5 6.7 %copy-start.7 = (s32[16,16]{1,0:T(8,128)S(1)}, s32[16,16]{1,0:T(8,128)}, u32[]{:S(2)}) copy-start(s32[16,16]{1,0:T(8,128)} %param.24) | copy-start | bytes 3076
  49.5 6.8 %copy-start.8 = (s32[16,16]{1,0:T(8,128)S(1)}, s32[16,16]{1,0:T(8,128)}, u32[]{:S(2)}) copy-start(s32[16,16]{1,0:T(8,128)} %param.23) | copy-start | bytes 3076
  50.4 10.5 %collective-permute-start = (bf16[16,16,1024]{2,0,1:T(8,128)(2,1)S(1)}, bf16[16,16,1024]{2,0,1:T(8,128)(2,1)S(1)}, u32[]{:S(2)}, u32[]{:S(2)}) collective-permute-start(bf16[16,16,1024]{2,0,1:T(8,128)(2,1)S(1)} %fusion.16), channel_id=1, source_target_pairs={{0,8},{8,16},{16,24},{24,32},{32,40},{40,48},{48,56},{56,64},{64,7... | collective-permute-start | bytes 1572872 | tf_op jit(solution)/shard_map/ppermute | solution.py:17
  52.3 10.3 %collective-permute-start.1 = (bf16[16,16,1024]{2,0,1:T(8,128)(2,1)S(1)}, bf16[16,16,1024]{2,0,1:T(8,128)(2,1)}, u32[]{:S(2)}, u32[]{:S(2)}) collective-permute-start(bf16[16,16,1024]{2,0,1:T(8,128)(2,1)S(1)} %fusion.16), channel_id=1, source_target_pairs={{8,0},{16,8},{24,16},{32,24},{40,32},{48,40},{56,48},{64,56},{72,6... | collective-permute-start | bytes 1572872 | tf_op jit(solution)/shard_map/ppermute | solution.py:19
  116.5 13.4 %copy-start.10 = (s32[4,8]{1,0:T(4,128)S(1)}, s32[4,8]{1,0:T(4,128)}, u32[]{:S(2)}) copy-start(s32[4,8]{1,0:T(4,128)} %param.17) | copy-start | bytes 388
  120.6 45.3 %copy-start.2 = (bf16[4,2,2,512,128]{4,3,2,1,0:T(8,128)(2,1)S(1)}, bf16[4,2,2,512,128]{4,3,2,1,0:T(8,128)(2,1)}, u32[]{:S(2)}) copy-start(bf16[4,2,2,512,128]{4,3,2,1,0:T(8,128)(2,1)} %param.15) | copy-start | bytes 6291460
  121.6 8.4 %collective-permute-start.2 = (bf16[4,8,128]{2,1,0:T(8,128)(2,1)S(1)}, bf16[4,8,128]{2,1,0:T(8,128)(2,1)S(1)}, u32[]{:S(2)}, u32[]{:S(2)}) collective-permute-start(bf16[4,8,128]{2,1,0:T(8,128)(2,1)S(1)} %copy-done.4), channel_id=1, source_target_pairs={{0,1},{1,2},{2,3},{3,4},{4,5},{5,6},{6,7},{7,8},{8,9},{9,10},{10,1... | collective-permute-start | bytes 24584 | tf_op jit(solution)/shard_map/ppermute | solution.py:17
  125.3 5.9 %collective-permute-start.3 = (bf16[4,8,128]{2,1,0:T(8,128)(2,1)S(1)}, bf16[4,8,128]{2,1,0:T(8,128)(2,1)S(1)}, u32[]{:S(2)}, u32[]{:S(2)}) collective-permute-start(bf16[4,8,128]{2,1,0:T(8,128)(2,1)S(1)} %copy-done.4), channel_id=1, source_target_pairs={{1,0},{2,1},{3,2},{4,3},{5,4},{6,5},{7,6},{8,7},{9,8},{10,9},{11,1... | collective-permute-start | bytes 24584 | tf_op jit(solution)/shard_map/ppermute | solution.py:19
  166.1 1.6 copy-start.3
Sparse Core Ops, SparseCore 0:
  121.7 43.2 reduce-scatter.1
where the time goes:
time: 177 us; the launch traced here: 176 us
  local copies, waits for them, and re-layouts  44.3 us (25%)
  waiting for transfers between devices  37.4 us (21%)
  blocking collectives  31.6 us (18%)
  matrix products  19.5 us (11%)
  other arithmetic  14.1 us (8%)
  starting transfers between devices  14 us (8%)
  between operations  13.8 us (8%)
    gather x16, local copies, waits for them, and re-layouts, add_entry(): jnp.take(padded, top_src[:, entry] - base_index, axis=0).astype(jnp.float32)  31.8 us
    all_gather x1, blocking collectives, per_device(): piece = lax.all_gather(patterns, 'samp', axis=0, tiled=True)  31.6 us
    reduce_scatter x1, waiting for transfers between devices, per_device(): lax.psum_scatter(folded.reshape(leaf_count * lax.axis_size('samp'), comps...  29.9 us
    dot_general x32, matrix products, contract(): jnp.einsum(form, first_op, second_op, preferred_element_type=jnp.float32)  14.6 us
    ppermute x2, starting transfers between devices, with_halo(): lax.ppermute(head, axis, [((i + 1) % count, i) for i in range(ends)])  8.4 us
    ppermute x2, starting transfers between devices, with_halo(): lax.ppermute(tail, axis, [(i, (i + 1) % count) for i in range(ends)])  5.61 us
    add x16, other arithmetic, add_entry(): return total + jnp.concatenate([part_real, part_imag], axis=1)  5.52 us
    ppermute x2, waiting for transfers between devices, with_halo(): lax.ppermute(tail, axis, [(i, (i + 1) % count) for i in range(ends)])  4.53 us
  transfers between devices with their start and end apart: 5, of which 4 were waited for; matrix products, arithmetic and copies ran while one was open for 2% of the time, Pallas kernels for 0%

commit v1 on v0

--- a/solution.py
+++ b/solution.py
@@ -75,7 +75,11 @@
         ],
         axis=1,
     ).astype(jnp.bfloat16)
-    piece = lax.all_gather(patterns, "samp", axis=0, tiled=True)
+    devices = lax.axis_size("samp")
+    repeats = [devices if d == 0 else 1 for d in range(patterns.ndim)]
+    piece = lax.all_to_all(
+        jnp.tile(patterns, repeats), "samp", split_axis=0, concat_axis=0, tiled=True
+    )
     piece_rows = piece.shape[0]
     picked = piece.reshape(piece_rows, comps, in_blocks, block_size)[:, :, interp_idx, :]
     moved_rows = contract("lcbri,brki->lcbk", picked, interp_val)

time: 177 us -> 171 us (0.966)
  blocking collectives: 31.6 us -> 0 us
  waiting for transfers between devices: 37.4 us -> 52.1 us
  starting transfers between devices: 14 us -> 23.8 us
    all_gather x1 -> x0, blocking collectives: 31.6 us -> none  [per_device(): piece = lax.all_gather(patterns, 'samp', axis=0, tiled=True)]
    all_to_all x0 -> x1, waiting for transfers between devices: none -> 16.5 us  [per_device(): lax.all_to_all(jnp.tile(patterns, repeats), 'samp', split_axis=0, concat_...]
    all_to_all x0 -> x1, starting transfers between devices: none -> 10.3 us  [per_device(): lax.all_to_all(jnp.tile(patterns, repeats), 'samp', split_axis=0, concat_...]
    unnamed x32 -> x34, local copies, waits for them, and re-layouts: 3.28 us -> 3.62 us
  transfers between devices with their start and end apart: 5 -> 6, of which waited for: 4 -> 5; matrix products, arithmetic and copies ran while one was open for 2% -> 3% of each run, Pallas kernels for 0% -> 0%
where the time goes in v1:
time: 171 us; the launch traced here: 170 us
  waiting for transfers between devices  52.1 us (30%)
  local copies, waits for them, and re-layouts  45.5 us (27%)
  starting transfers between devices  23.8 us (14%)
  matrix products  19.4 us (11%)
  other arithmetic  14.5 us (8%)
  between operations  13.8 us (8%)
    gather x16, local copies, waits for them, and re-layouts, add_entry(): jnp.take(padded, top_src[:, entry] - base_index, axis=0).astype(jnp.float32)  31.8 us
    reduce_scatter x1, waiting for transfers between devices, per_device(): lax.psum_scatter(folded.reshape(leaf_count * lax.axis_size('samp'), comps...  28.2 us
    all_to_all x1, waiting for transfers between devices, per_device(): lax.all_to_all(jnp.tile(patterns, repeats), 'samp', split_axis=0, concat_...  16.5 us
    dot_general x32, matrix products, contract(): jnp.einsum(form, first_op, second_op, preferred_element_type=jnp.float32)  14.5 us
    all_to_all x1, starting transfers between devices, per_device(): lax.all_to_all(jnp.tile(patterns, repeats), 'samp', split_axis=0, concat_...  10.3 us
    ppermute x2, starting transfers between devices, with_halo(): lax.ppermute(head, axis, [((i + 1) % count, i) for i in range(ends)])  9.02 us
    add x16, other arithmetic, add_entry(): return total + jnp.concatenate([part_real, part_imag], axis=1)  5.52 us
    ppermute x2, waiting for transfers between devices, with_halo(): lax.ppermute(tail, axis, [(i, (i + 1) % count) for i in range(ends)])  4.53 us
  transfers between devices with their start and end apart: 6, of which 5 were waited for; matrix products, arithmetic and copies ran while one was open for 3% of the time, Pallas kernels for 0%

profile of v1, /device:TPU:2, one launch (start us, length us, event | category | flops | bytes accessed | tf_op | source)
XLA Modules:
  0.0 170.4 jit_solution(2698245693902373581)
XLA Ops:
  6.5 1.8 %fusion.46 = f32[4,4,2,512]{3,1,2,0:T(4,128)S(1)} fusion(bf16[4,2,2,512,128]{4,3,2,1,0:T(8,128)(2,1)} %param.15, bf16[4,8,128]{2,1,0:T(8,128)(2,1)} %param.14), kind=kOutput, calls=%fused_computation.65 | convolution fusion | flops 4194304 | bytes 1118208 | tf_op jit(solution)/shard_map/lpqu,leu->lpeq/dot_general | solution.py:31
  8.3 1.6 fusion.44
  11.7 10.3 %all-to-all-start = ((bf16[32,16,512]{2,1,0:T(8,128)(2,1)}), bf16[32,16,512]{2,1,0:T(8,128)(2,1)S(1)}, u32[]{:S(2)}, u32[]{:S(2)}) async-start(bf16[32,16,512]{2,1,0:T(8,128)(2,1)} %bitcast.15), calls=%async_computation | async-start | bytes 1048576 | tf_op jit(solution)/shard_map/all_to_all | solution.py:80
  23.1 16.5 %all-to-all-done = bf16[32,16,512]{2,1,0:T(8,128)(2,1)S(1)} async-done(((bf16[32,16,512]{2,1,0:T(8,128)(2,1)}), bf16[32,16,512]{2,1,0:T(8,128)(2,1)S(1)}, u32[]{:S(2)}, u32[]{:S(2)}) %all-to-all-start) | async-done | bytes 524320 | tf_op jit(solution)/shard_map/all_to_all | solution.py:80
  41.4 2.6 %copy.73 = f32[32,16,8,128]{3,2,0,1:T(8,128)} copy(f32[32,16,8,128]{3,1,0,2:T(8,128)S(1)} %convolution_bitcast_fusion.1) | data formatting | bytes 4194304 | tf_op jit(solution)/shard_map/reshape | solution.py:86
  44.0 1.7 %reshape.110 = f32[32,16,1024]{2,0,1:T(8,128)S(1)} reshape(f32[32,16,8,128]{3,2,0,1:T(8,128)} %copy.73) | data formatting | bytes 4194304 | tf_op jit(solution)/shard_map/reshape | solution.py:86
  47.2 1.9 %collective-permute-start = (bf16[16,16,1024]{2,0,1:T(8,128)(2,1)S(1)}, bf16[16,16,1024]{2,0,1:T(8,128)(2,1)S(1)}, u32[]{:S(2)}, u32[]{:S(2)}) collective-permute-start(bf16[16,16,1024]{2,0,1:T(8,128)(2,1)S(1)} %fusion.16), channel_id=1, source_target_pairs={{0,8},{8,16},{16,24},{24,32},{32,40},{40,48},{48,56},{56,64},{64,7... | collective-permute-start | bytes 1572872 | tf_op jit(solution)/shard_map/ppermute | solution.py:17
  49.1 3.8 %collective-permute-start.1 = (bf16[16,16,1024]{2,0,1:T(8,128)(2,1)S(1)}, bf16[16,16,1024]{2,0,1:T(8,128)(2,1)}, u32[]{:S(2)}, u32[]{:S(2)}) collective-permute-start(bf16[16,16,1024]{2,0,1:T(8,128)(2,1)S(1)} %fusion.16), channel_id=1, source_target_pairs={{8,0},{16,8},{24,16},{32,24},{40,32},{48,40},{56,48},{64,56},{72,6... | collective-permute-start | bytes 1572872 | tf_op jit(solution)/shard_map/ppermute | solution.py:19
  53.1 4.5 %collective-permute-done = bf16[16,16,1024]{2,0,1:T(8,128)(2,1)S(1)} collective-permute-done((bf16[16,16,1024]{2,0,1:T(8,128)(2,1)S(1)}, bf16[16,16,1024]{2,0,1:T(8,128)(2,1)S(1)}, u32[]{:S(2)}, u32[]{:S(2)}) %collective-permute-start) | collective-permute-done | bytes 524320 | tf_op jit(solution)/shard_map/ppermute | solution.py:17
  57.7 1.8 %collective-permute-done.1 = bf16[16,16,1024]{2,0,1:T(8,128)(2,1)} collective-permute-done((bf16[16,16,1024]{2,0,1:T(8,128)(2,1)S(1)}, bf16[16,16,1024]{2,0,1:T(8,128)(2,1)}, u32[]{:S(2)}, u32[]{:S(2)}) %collective-permute-start.1) | collective-permute-done | bytes 524320 | tf_op jit(solution)/shard_map/ppermute | solution.py:19
  60.6 2.1 %copy.51 = bf16[48,16,1024]{2,1,0:T(8,128)(2,1)} copy(bf16[48,16,1024]{2,0,1:T(8,128)(2,1)S(1)} %pad_maximum_fusion) | data formatting | bytes 3145728
  62.7 48.1 %while.14 = (s32[]{:T(128)}, f32[16,16,1024]{2,1,0:T(8,128)S(1)}, s32[16,16]{0,1:T(8,128)S(1)}, bf16[32,2,1024]{2,0,1:T(8,128)(2,1)S(1)}, s32[16,16]{0,1:T(8,128...) while((s32[]{:T(128)}, f32[16,16,1024]{2,1,0:T(8,128)S(1)}, ...), condition=%wide.region_1.0_spmd.clone, body=%wide.region_0.1_spmd.clone.sunk | while | flops 4195955 | bytes 8524371 | solution.py:117
  62.7 2.0 %gather_fusion = bf16[16,16,1024]{2,1,0:T(8,128)(2,1)S(1)} fusion(bf16[48,16,1024]{2,1,0:T(8,128)(2,1)} %get-tuple-element.285, s32[1024]{0:T(1024)S(1)} %pad_clamp_fusion.4), kind=kCustom, calls=%fused_computation.clone.clone.1 | custom fusion | bytes 1048640 | tf_op jit(solution)/shard_map/while/body/eval_jaxpr/jit(_take)/gather | solution.py:107
  65.7 2.0 %gather_fusion = bf16[16,16,1024]{2,1,0:T(8,128)(2,1)S(1)} fusion(bf16[48,16,1024]{2,1,0:T(8,128)(2,1)} %get-tuple-element.285, s32[1024]{0:T(1024)S(1)} %pad_clamp_fusion.4), kind=kCustom, calls=%fused_computation.clone.clone.1 | custom fusion | bytes 1048640 | tf_op jit(solution)/shard_map/while/body/eval_jaxpr/jit(_take)/gather | solution.py:107
  68.7 2.0 %gather_fusion = bf16[16,16,1024]{2,1,0:T(8,128)(2,1)S(1)} fusion(bf16[48,16,1024]{2,1,0:T(8,128)(2,1)} %get-tuple-element.285, s32[1024]{0:T(1024)S(1)} %pad_clamp_fusion.4), kind=kCustom, calls=%fused_computation.clone.clone.1 | custom fusion | bytes 1048640 | tf_op jit(solution)/shard_map/while/body/eval_jaxpr/jit(_take)/gather | solution.py:107
  71.7 2.0 %gather_fusion = bf16[16,16,1024]{2,1,0:T(8,128)(2,1)S(1)} fusion(bf16[48,16,1024]{2,1,0:T(8,128)(2,1)} %get-tuple-element.285, s32[1024]{0:T(1024)S(1)} %pad_clamp_fusion.4), kind=kCustom, calls=%fused_computation.clone.clone.1 | custom fusion | bytes 1048640 | tf_op jit(solution)/shard_map/while/body/eval_jaxpr/jit(_take)/gather | solution.py:107
  74.7 2.0 %gather_fusion = bf16[16,16,1024]{2,1,0:T(8,128)(2,1)S(1)} fusion(bf16[48,16,1024]{2,1,0:T(8,128)(2,1)} %get-tuple-element.285, s32[1024]{0:T(1024)S(1)} %pad_clamp_fusion.4), kind=kCustom, calls=%fused_computation.clone.clone.1 | custom fusion | bytes 1048640 | tf_op jit(solution)/shard_map/while/body/eval_jaxpr/jit(_take)/gather | solution.py:107
  77.7 2.0 %gather_fusion = bf16[16,16,1024]{2,1,0:T(8,128)(2,1)S(1)} fusion(bf16[48,16,1024]{2,1,0:T(8,128)(2,1)} %get-tuple-element.285, s32[1024]{0:T(1024)S(1)} %pad_clamp_fusion.4), kind=kCustom, calls=%fused_computation.clone.clone.1 | custom fusion | bytes 1048640 | tf_op jit(solution)/shard_map/while/body/eval_jaxpr/jit(_take)/gather | solution.py:107
  80.7 2.0 %gather_fusion = bf16[16,16,1024]{2,1,0:T(8,128)(2,1)S(1)} fusion(bf16[48,16,1024]{2,1,0:T(8,128)(2,1)} %get-tuple-element.285, s32[1024]{0:T(1024)S(1)} %pad_clamp_fusion.4), kind=kCustom, calls=%fused_computation.clone.clone.1 | custom fusion | bytes 1048640 | tf_op jit(solution)/shard_map/while/body/eval_jaxpr/jit(_take)/gather | solution.py:107
  83.7 2.0 %gather_fusion = bf16[16,16,1024]{2,1,0:T(8,128)(2,1)S(1)} fusion(bf16[48,16,1024]{2,1,0:T(8,128)(2,1)} %get-tuple-element.285, s32[1024]{0:T(1024)S(1)} %pad_clamp_fusion.4), kind=kCustom, calls=%fused_computation.clone.clone.1 | custom fusion | bytes 1048640 | tf_op jit(solution)/shard_map/while/body/eval_jaxpr/jit(_take)/gather | solution.py:107
  86.7 2.0 %gather_fusion = bf16[16,16,1024]{2,1,0:T(8,128)(2,1)S(1)} fusion(bf16[48,16,1024]{2,1,0:T(8,128)(2,1)} %get-tuple-element.285, s32[1024]{0:T(1024)S(1)} %pad_clamp_fusion.4), kind=kCustom, calls=%fused_computation.clone.clone.1 | custom fusion | bytes 1048640 | tf_op jit(solution)/shard_map/while/body/eval_jaxpr/jit(_take)/gather | solution.py:107
  89.7 2.0 %gather_fusion = bf16[16,16,1024]{2,1,0:T(8,128)(2,1)S(1)} fusion(bf16[48,16,1024]{2,1,0:T(8,128)(2,1)} %get-tuple-element.285, s32[1024]{0:T(1024)S(1)} %pad_clamp_fusion.4), kind=kCustom, calls=%fused_computation.clone.clone.1 | custom fusion | bytes 1048640 | tf_op jit(solution)/shard_map/while/body/eval_jaxpr/jit(_take)/gather | solution.py:107
  92.7 2.0 %gather_fusion = bf16[16,16,1024]{2,1,0:T(8,128)(2,1)S(1)} fusion(bf16[48,16,1024]{2,1,0:T(8,128)(2,1)} %get-tuple-element.285, s32[1024]{0:T(1024)S(1)} %pad_clamp_fusion.4), kind=kCustom, calls=%fused_computation.clone.clone.1 | custom fusion | bytes 1048640 | tf_op jit(solution)/shard_map/while/body/eval_jaxpr/jit(_take)/gather | solution.py:107
  95.7 2.0 %gather_fusion = bf16[16,16,1024]{2,1,0:T(8,128)(2,1)S(1)} fusion(bf16[48,16,1024]{2,1,0:T(8,128)(2,1)} %get-tuple-element.285, s32[1024]{0:T(1024)S(1)} %pad_clamp_fusion.4), kind=kCustom, calls=%fused_computation.clone.clone.1 | custom fusion | bytes 1048640 | tf_op jit(solution)/shard_map/while/body/eval_jaxpr/jit(_take)/gather | solution.py:107
  98.8 2.0 %gather_fusion = bf16[16,16,1024]{2,1,0:T(8,128)(2,1)S(1)} fusion(bf16[48,16,1024]{2,1,0:T(8,128)(2,1)} %get-tuple-element.285, s32[1024]{0:T(1024)S(1)} %pad_clamp_fusion.4), kind=kCustom, calls=%fused_computation.clone.clone.1 | custom fusion | bytes 1048640 | tf_op jit(solution)/shard_map/while/body/eval_jaxpr/jit(_take)/gather | solution.py:107
  101.8 2.0 %gather_fusion = bf16[16,16,1024]{2,1,0:T(8,128)(2,1)S(1)} fusion(bf16[48,16,1024]{2,1,0:T(8,128)(2,1)} %get-tuple-element.285, s32[1024]{0:T(1024)S(1)} %pad_clamp_fusion.4), kind=kCustom, calls=%fused_computation.clone.clone.1 | custom fusion | bytes 1048640 | tf_op jit(solution)/shard_map/while/body/eval_jaxpr/jit(_take)/gather | solution.py:107
  104.8 2.0 %gather_fusion = bf16[16,16,1024]{2,1,0:T(8,128)(2,1)S(1)} fusion(bf16[48,16,1024]{2,1,0:T(8,128)(2,1)} %get-tuple-element.285, s32[1024]{0:T(1024)S(1)} %pad_clamp_fusion.4), kind=kCustom, calls=%fused_computation.clone.clone.1 | custom fusion | bytes 1048640 | tf_op jit(solution)/shard_map/while/body/eval_jaxpr/jit(_take)/gather | solution.py:107
  107.8 2.0 %gather_fusion = bf16[16,16,1024]{2,1,0:T(8,128)(2,1)S(1)} fusion(bf16[48,16,1024]{2,1,0:T(8,128)(2,1)} %get-tuple-element.285, s32[1024]{0:T(1024)S(1)} %pad_clamp_fusion.4), kind=kCustom, calls=%fused_computation.clone.clone.1 | custom fusion | bytes 1048640 | tf_op jit(solution)/shard_map/while/body/eval_jaxpr/jit(_take)/gather | solution.py:107
  113.3 4.1 %fusion.19 = bf16[32,16,4,128]{3,2,1,0:T(4,128)(2,1)S(1)} fusion(f32[32,16,8,2,128]{4,1,3,0,2:T(8,128)S(1)} %convolution_bitcast_fusion, s32[8,2]{0,1:T(2,128)S(1)} %copy-done.9), kind=kOutput, calls=%fused_computation.29 | convolution fusion | flops 50593856 | bytes 4718656 | tf_op jit(solution)/shard_map/lcbri,brq->lcqi/dot_general | solution.py:133
  118.4 2.5 %collective-permute-start.2 = (bf16[4,8,128]{2,1,0:T(8,128)(2,1)S(1)}, bf16[4,8,128]{2,1,0:T(8,128)(2,1)S(1)}, u32[]{:S(2)}, u32[]{:S(2)}) collective-permute-start(bf16[4,8,128]{2,1,0:T(8,128)(2,1)S(1)} %copy-done.4), channel_id=1, source_target_pairs={{0,1},{1,2},{2,3},{3,4},{4,5},{5,6},{6,7},{7,8},{8,9},{9,10},{10,1... | collective-permute-start | bytes 24584 | tf_op jit(solution)/shard_map/ppermute | solution.py:17
  120.9 5.2 %collective-permute-start.3 = (bf16[4,8,128]{2,1,0:T(8,128)(2,1)S(1)}, bf16[4,8,128]{2,1,0:T(8,128)(2,1)S(1)}, u32[]{:S(2)}, u32[]{:S(2)}) collective-permute-start(bf16[4,8,128]{2,1,0:T(8,128)(2,1)S(1)} %copy-done.4), channel_id=1, source_target_pairs={{1,0},{2,1},{3,2},{4,3},{5,4},{6,5},{7,6},{8,7},{9,8},{10,9},{11,1... | collective-permute-start | bytes 24584 | tf_op jit(solution)/shard_map/ppermute | solution.py:19
  131.4 28.2 %reduce-scatter.2.cloned.1.call-done = bf16[4,16,512]{2,1,0:T(8,128)(2,1)} async-done(((bf16[32,16,512]{2,1,0:T(8,128)(2,1)}), bf16[4,16,512]{2,1,0:T(8,128)(2,1)}) %reduce-scatter.2.cloned.1.call-update) | async-done | bytes 65552 | tf_op jit(solution)/shard_map/reduce_scatter | solution.py:134
  (210 shorter events, 35.2 us)
Async XLA Ops:
  6.5 34.2 %copy-start = (bf16[8,2,128,128]{3,2,1,0:T(8,128)(2,1)S(1)}, bf16[8,2,128,128]{3,2,1,0:T(8,128)(2,1)}, u32[]{:S(2)}) copy-start(bf16[8,2,128,128]{3,2,1,0:T(8,128)(2,1)} %param.22) | copy-start | bytes 1572868
  6.5 3.4 %copy-start.4 = (bf16[4,8,128]{2,1,0:T(8,128)(2,1)S(1)}, bf16[4,8,128]{2,1,0:T(8,128)(2,1)}, u32[]{:S(2)}) copy-start(bf16[4,8,128]{2,1,0:T(8,128)(2,1)} %param.14) | copy-start | bytes 24580
  6.5 3.4 %copy-start.1 = (bf16[4,2,2,512,128]{4,3,2,1,0:T(8,128)(2,1)S(1)}, bf16[4,2,2,512,128]{4,3,2,1,0:T(8,128)(2,1)}, u32[]{:S(2)}) copy-start(bf16[4,2,2,512,128]{4,3,2,1,0:T(8,128)(2,1)} %param.15) | copy-start | bytes 6291460
  9.9 12.1 %copy-start.9 = (s32[8,2]{0,1:T(2,128)S(1)}, s32[8,2]{0,1:T(2,128)}, u32[]{:S(2)}) copy-start(s32[8,2]{0,1:T(2,128)} %param.21) | copy-start | bytes 196
  10.0 12.3 %copy-start.13 = (s32[32]{0:T(128)S(1)}, s32[32]{0:T(128)}, u32[]{:S(2)}) copy-start(s32[32]{0:T(128)} %param.18) | copy-start | bytes 388
  10.0 12.8 %copy-start.6 = (bf16[8,2,1024]{2,1,0:T(2,128)(2,1)S(1)}, bf16[8,2,1024]{2,1,0:T(2,128)(2,1)}, u32[]{:S(2)}) copy-start(bf16[8,2,1024]{2,1,0:T(2,128)(2,1)} %param.20) | copy-start | bytes 98308
  10.0 12.8 %copy-start.12 = (s32[32]{0:T(128)S(1)}, s32[32]{0:T(128)}, u32[]{:S(2)}) copy-start(s32[32]{0:T(128)} %param.19) | copy-start | bytes 388
  11.7 27.8 %all-to-all-start = ((bf16[32,16,512]{2,1,0:T(8,128)(2,1)}), bf16[32,16,512]{2,1,0:T(8,128)(2,1)S(1)}, u32[]{:S(2)}, u32[]{:S(2)}) async-start(bf16[32,16,512]{2,1,0:T(8,128)(2,1)} %bitcast.15), calls=%async_computation | async-start | bytes 1048576 | tf_op jit(solution)/shard_map/all_to_all | solution.py:80
  22.0 137.5 %reduce-scatter.2.cloned.1.call-start = ((), (), s32[]{:S(2)}) async-start(), calls=%async_computation.2 | async-start | bytes 589824 | tf_op jit(solution)/shard_map/reduce_scatter | solution.py:134
  45.7 0.7 copy-start.11
  46.0 7.0 %copy-start.5 = (bf16[32,2,1024]{2,1,0:T(2,128)(2,1)S(1)}, bf16[32,2,1024]{2,1,0:T(2,128)(2,1)}, u32[]{:S(2)}) copy-start(bf16[32,2,1024]{2,1,0:T(2,128)(2,1)} %param.25) | copy-start | bytes 393220
  46.0 7.0 %copy-start.7 = (s32[16,16]{1,0:T(8,128)S(1)}, s32[16,16]{1,0:T(8,128)}, u32[]{:S(2)}) copy-start(s32[16,16]{1,0:T(8,128)} %param.24) | copy-start | bytes 3076
  46.0 7.1 %copy-start.8 = (s32[16,16]{1,0:T(8,128)S(1)}, s32[16,16]{1,0:T(8,128)}, u32[]{:S(2)}) copy-start(s32[16,16]{1,0:T(8,128)} %param.23) | copy-start | bytes 3076
  47.2 10.5 %collective-permute-start = (bf16[16,16,1024]{2,0,1:T(8,128)(2,1)S(1)}, bf16[16,16,1024]{2,0,1:T(8,128)(2,1)S(1)}, u32[]{:S(2)}, u32[]{:S(2)}) collective-permute-start(bf16[16,16,1024]{2,0,1:T(8,128)(2,1)S(1)} %fusion.16), channel_id=1, source_target_pairs={{0,8},{8,16},{16,24},{24,32},{32,40},{40,48},{48,56},{56,64},{64,7... | collective-permute-start | bytes 1572872 | tf_op jit(solution)/shard_map/ppermute | solution.py:17
  49.1 10.3 %collective-permute-start.1 = (bf16[16,16,1024]{2,0,1:T(8,128)(2,1)S(1)}, bf16[16,16,1024]{2,0,1:T(8,128)(2,1)}, u32[]{:S(2)}, u32[]{:S(2)}) collective-permute-start(bf16[16,16,1024]{2,0,1:T(8,128)(2,1)S(1)} %fusion.16), channel_id=1, source_target_pairs={{8,0},{16,8},{24,16},{32,24},{40,32},{48,40},{56,48},{64,56},{72,6... | collective-permute-start | bytes 1572872 | tf_op jit(solution)/shard_map/ppermute | solution.py:19
  113.3 12.8 %copy-start.10 = (s32[4,8]{1,0:T(4,128)S(1)}, s32[4,8]{1,0:T(4,128)}, u32[]{:S(2)}) copy-start(s32[4,8]{1,0:T(4,128)} %param.17) | copy-start | bytes 388
  117.4 43.0 %copy-start.2 = (bf16[4,2,2,512,128]{4,3,2,1,0:T(8,128)(2,1)S(1)}, bf16[4,2,2,512,128]{4,3,2,1,0:T(8,128)(2,1)}, u32[]{:S(2)}) copy-start(bf16[4,2,2,512,128]{4,3,2,1,0:T(8,128)(2,1)} %param.15) | copy-start | bytes 6291460
  118.4 7.8 %collective-permute-start.2 = (bf16[4,8,128]{2,1,0:T(8,128)(2,1)S(1)}, bf16[4,8,128]{2,1,0:T(8,128)(2,1)S(1)}, u32[]{:S(2)}, u32[]{:S(2)}) collective-permute-start(bf16[4,8,128]{2,1,0:T(8,128)(2,1)S(1)} %copy-done.4), channel_id=1, source_target_pairs={{0,1},{1,2},{2,3},{3,4},{4,5},{5,6},{6,7},{7,8},{8,9},{9,10},{10,1... | collective-permute-start | bytes 24584 | tf_op jit(solution)/shard_map/ppermute | solution.py:17
  120.9 6.6 %collective-permute-start.3 = (bf16[4,8,128]{2,1,0:T(8,128)(2,1)S(1)}, bf16[4,8,128]{2,1,0:T(8,128)(2,1)S(1)}, u32[]{:S(2)}, u32[]{:S(2)}) collective-permute-start(bf16[4,8,128]{2,1,0:T(8,128)(2,1)S(1)} %copy-done.4), channel_id=1, source_target_pairs={{1,0},{2,1},{3,2},{4,3},{5,4},{6,5},{7,6},{8,7},{9,8},{10,9},{11,1... | collective-permute-start | bytes 24584 | tf_op jit(solution)/shard_map/ppermute | solution.py:19
  160.6 1.6 copy-start.3
Sparse Core Ops, SparseCore 0:
  118.5 40.9 reduce-scatter.1
